TPU v7x, 32 devices: a whole 2x2x4 slice. The times are simulated.
32 devices in a mesh: dom: 4 (over y, x), fsdp: 8 (over z, core).
Axes of the slice: x: 2, y: 2, z: 4, core: 2. Of those that a mesh axis runs over, the one named last changes fastest.
Arguments:
- inputs: bfloat16 [4, 1024, 4096], P('dom', 'fsdp'), may hold values from -6 to 6
- cotangent: bfloat16 [4, 1024, 8192], P('dom', 'fsdp'), may hold values from -6 to 6
- shared_weight: bfloat16 [4096, 8192], P(None, 'fsdp'), may hold values from -0.09375 to 0.09375
- domain_weight: bfloat16 [4, 4096, 8192], P('dom', None, 'fsdp'), may hold values from 0.099609375 to 1.8984375
- row_counts: int32 [4], P('dom'), may hold values from 65 to 1024, as said below
Outputs:
- shared_grad: float32 [4096, 8192], P('dom', 'fsdp')
- domain_grad: bfloat16 [4, 4096, 8192], P('dom', None, 'fsdp')
- input_grad: bfloat16 [4, 1024, 4096], P('dom', 'fsdp')
Inputs may be any that keep to these rules, and one draw needn't show every extreme that they name: `row_counts`: rows of a domain at positions from its count on are padding. Some domain is full in every draw.
All inputs are finite; a program needn't handle non-finite values.
Results may differ from a plain program's by a relative error of at most 0.017.
Values may be sent and summed in bfloat16 or wider, within the bound.
A program may use at most 128 MiB of HBM per device.

v0:
```python
import jax
import jax.numpy as jnp
from jax import lax
from jax.sharding import PartitionSpec as P


def body(inputs, cotangent, shared_weight, domain_weight, row_counts):
    effective = (shared_weight.astype(jnp.float32) * domain_weight[0].astype(jnp.float32)).astype(
        jnp.bfloat16
    )
    live_rows = row_counts[0]
    columns = lax.all_to_all(cotangent[0], "fsdp", split_axis=1, concat_axis=0, tiled=True)
    piece = lax.all_gather(inputs[0], "fsdp", axis=0, tiled=True)
    length = piece.shape[0]
    upstream = columns.astype(jnp.float32)
    preact = jnp.dot(piece, effective, preferred_element_type=jnp.float32)
    sigma = jax.nn.sigmoid(preact)
    position = lax.iota(jnp.int32, length)
    slope = upstream * sigma * (1.0 + preact * (1.0 - sigma))
    fold_grad_pre = jnp.where((position < live_rows)[:, None], slope, jnp.float32(0.0)).astype(
        jnp.bfloat16
    )
    weight_sum = lax.dot_general(
        piece, fold_grad_pre, (((0,), (0,)), ((), ())), preferred_element_type=jnp.float32
    )
    weight_sum, grad_pre = (weight_sum, fold_grad_pre)
    scaled = weight_sum * lax.rsqrt(live_rows.astype(jnp.float32))
    input_grad = lax.psum_scatter(
        lax.dot_general(
            grad_pre, effective, (((1,), (1,)), ((), ())), preferred_element_type=jnp.float32
        ).astype(jnp.bfloat16),
        "fsdp",
        scatter_dimension=0,
        tiled=True,
    )
    shared_grad = lax.psum_scatter(
        (scaled * domain_weight[0].astype(jnp.float32)).astype(jnp.bfloat16),
        "dom",
        scatter_dimension=0,
        tiled=True,
    ).astype(jnp.float32)
    domain_grad = (scaled * shared_weight.astype(jnp.float32)).astype(jnp.bfloat16)
    return (shared_grad, domain_grad[None], input_grad[None])


def solution(mesh):
    return jax.shard_map(
        body,
        mesh=mesh,
        in_specs=(
            P("dom", "fsdp", None),
            P("dom", "fsdp", None),
            P(None, "fsdp"),
            P("dom", None, "fsdp"),
            P("dom"),
        ),
        out_specs=(P("dom", "fsdp"), P("dom", None, "fsdp"), P("dom", "fsdp", None)),
        check_vma=False,
    )
```

profile of v0, /device:TPU:0, one launch (start us, length us, event | category | flops | bytes accessed | tf_op | source)
XLA Modules:
  0.0 358.8 jit_solution(8678285528174618740)
XLA Ops:
  7.2 0.0 all-gather.3.cloned.1.call-start
  7.2 0.7 all-gather.3.cloned.1.call-update
  7.9 4.1 %copy.13 = bf16[1,128,8192]{1,2,0:T(8,128)(2,1)} copy(bf16[1,128,8192]{2,1,0:T(8,128)(2,1)} %param.6) | data formatting | bytes 4194304 | tf_op args[1]
  12.0 6.4 %all-to-all-start = ((bf16[128,8,1024]{0,2,1:T(8,128)(2,1)}), bf16[128,8,1024]{0,2,1:T(8,128)(2,1)S(1)}, u32[]{:S(2)}, u32[]{:S(2)}) async-start(bf16[128,8,1024]{0,2,1:T(8,128)(2,1)} %bitcast.1), calls=%async_computation | async-start | bytes 4194304 | tf_op jit(solution)/shard_map/all_to_all | solution.py:12
  18.3 0.0 reduce-scatter.3.cloned.1.call-start
  19.1 11.3 %copy.15 = bf16[4096,1024]{0,1:T(8,128)(2,1)} copy(bf16[4096,1024]{1,0:T(8,128)(2,1)} %param.7) | data formatting | bytes 16777216 | tf_op args[2]
  30.4 11.3 %copy.16 = bf16[1,4096,1024]{1,2,0:T(8,128)(2,1)} copy(bf16[1,4096,1024]{2,1,0:T(8,128)(2,1)} %param.8) | data formatting | bytes 16777216 | tf_op args[3]
  41.6 81.1 %all-to-all-done = bf16[128,8,1024]{0,2,1:T(8,128)(2,1)S(1)} async-done(((bf16[128,8,1024]{0,2,1:T(8,128)(2,1)}), bf16[128,8,1024]{0,2,1:T(8,128)(2,1)S(1)}, u32[]{:S(2)}, u32[]{:S(2)}) %all-to-all-start) | async-done | bytes 2097184 | tf_op jit(solution)/shard_map/all_to_all | solution.py:12
  122.7 13.7 %all-gather.3.cloned.1.call-done = bf16[1,1024,4096]{2,1,0:T(8,128)(2,1)} async-done(((bf16[1,128,4096]{2,1,0:T(8,128)(2,1)}), bf16[1,1024,4096]{2,1,0:T(8,128)(2,1)}) %all-gather.3.cloned.1.call-update) | async-done | bytes 8388624 | tf_op jit(solution)/shard_map/all_gather | solution.py:13
  136.4 17.1 %fusion.10 = bf16[1024,1024]{0,1:T(8,128)(2,1)} fusion(bf16[1,1024,4096]{2,1,0:T(8,128)(2,1)} %all-gather.3.cloned.1.call-done, bf16[4096,1024]{0,1:T(8,128)(2,1)} %copy.15, bf16[1,4096,1024]{1,2,0:T(8,128)(2,1)} %copy.16, pred[1024]{0:T(1024)(128)(4,1)S(1)} %iota_compare_fusion, bf16[128,8,1024]{0,2,1:T(8,128)(2,1)S(1)} %all-to-all-done), kind=kOutput, calls=%fused_computation.15 | convolution fusion | flops 8618246144 | bytes 29361152 | tf_op jit(solution)/shard_map/dot_general | solution.py:16
  153.5 20.9 %fusion.3 = (bf16[1,4096,1024]{1,2,0:T(8,128)(2,1)}, bf16[4096,1024]{0,1:T(8,128)(2,1)}) fusion(bf16[4096,1024]{0,1:T(8,128)(2,1)} %copy.15, f32[]{:T(128)S(6)} %rsqrt.3, bf16[1,4096,1024]{1,2,0:T(8,128)(2,1)} %copy.16, bf16[1024,1024]{0,1:T(8,128)(2,1)} %fusion.10, bf16[1,1024,4096]{2,1,0:T(8,128)(2,1)} %all-gather.3.cloned.1.call-done), kind=kOutput, calls=%fused_computation.6 | convolution fusion | flops 8619294720 | bytes 44040196 | tf_op jit(solution)/shard_map/dot_general | solution.py:23
  174.4 0.0 copy-start
  174.4 0.0 reduce-scatter.3.cloned.1.call-update
  174.5 0.2 reduce-scatter.5.cloned.1.call-start
  174.7 1.3 copy-done
  176.0 17.8 %convolution_convert_fusion = bf16[1024,4096]{1,0:T(8,128)(2,1)} fusion(bf16[1024,1024]{0,1:T(8,128)(2,1)S(1)} %copy-done, bf16[4096,1024]{0,1:T(8,128)(2,1)} %copy.15, bf16[1,4096,1024]{1,2,0:T(8,128)(2,1)} %copy.16), kind=kOutput, calls=%fused_computation.11 | convolution fusion | flops 8610906112 | bytes 27262976 | tf_op jit(solution)/shard_map/dot_general | solution.py:29
  193.8 0.0 reduce-scatter.5.cloned.1.call-update
  193.9 12.0 %copy.18 = bf16[1,4096,1024]{2,1,0:T(8,128)(2,1)} copy(bf16[1,4096,1024]{1,2,0:T(8,128)(2,1)} %get-tuple-element.9) | data formatting | bytes 16777216
  205.9 54.0 %reduce-scatter.3.cloned.1.call-done = bf16[1024,1024]{0,1:T(8,128)(2,1)} async-done(((bf16[4096,1024]{0,1:T(8,128)(2,1)}), bf16[1024,1024]{0,1:T(8,128)(2,1)}) %reduce-scatter.3.cloned.1.call-update) | async-done | bytes 2097168 | tf_op jit(solution)/shard_map/reduce_scatter | solution.py:36
  259.8 4.1 %copy.17 = f32[1024,1024]{1,0:T(8,128)} copy(bf16[1024,1024]{0,1:T(8,128)(2,1)} %reduce-scatter.3.cloned.1.call-done) | data formatting | bytes 6291456
  263.9 88.3 %reduce-scatter.5.cloned.1.call-done = bf16[128,4096]{1,0:T(8,128)(2,1)} async-done(((bf16[1024,4096]{1,0:T(8,128)(2,1)}), bf16[128,4096]{1,0:T(8,128)(2,1)}) %reduce-scatter.5.cloned.1.call-update) | async-done | bytes 1048592 | tf_op jit(solution)/shard_map/reduce_scatter | solution.py:28
  (1 shorter events, 0.0 us)
Async XLA Ops:
  7.2 129.2 %all-gather.3.cloned.1.call-start = ((), (), s32[]{:S(2)}) async-start(), calls=%async_computation.5 | async-start | bytes 9437184 | tf_op jit(solution)/shard_map/all_gather | solution.py:13
  12.0 110.8 %all-to-all-start = ((bf16[128,8,1024]{0,2,1:T(8,128)(2,1)}), bf16[128,8,1024]{0,2,1:T(8,128)(2,1)S(1)}, u32[]{:S(2)}, u32[]{:S(2)}) async-start(bf16[128,8,1024]{0,2,1:T(8,128)(2,1)} %bitcast.1), calls=%async_computation | async-start | bytes 4194304 | tf_op jit(solution)/shard_map/all_to_all | solution.py:12
  18.3 241.5 %reduce-scatter.3.cloned.1.call-start = ((), (), s32[]{:S(2)}) async-start(), calls=%async_computation.3 | async-start | bytes 10485760 | tf_op jit(solution)/shard_map/reduce_scatter | solution.py:36
  174.4 1.6 copy-start
  174.5 177.8 %reduce-scatter.5.cloned.1.call-start = ((), (), s32[]{:S(2)}) async-start(), calls=%async_computation.4 | async-start | bytes 9437184 | tf_op jit(solution)/shard_map/reduce_scatter | solution.py:28
Sparse Core Ops, SparseCore 0:
  9.6 126.7 all-gather.2
  174.6 85.2 reduce-scatter.2
  262.7 89.5 reduce-scatter.4
where the time goes:
time: 360 us; the launch traced here: 359 us
  waiting for transfers between devices  238 us (66%)
  matrix products  55.8 us (16%)
  local copies, waits for them, and re-layouts  44.1 us (12%)
  between operations  14.4 us (4%)
  starting transfers between devices  6.65 us (2%)
    reduce_scatter x1, waiting for transfers between devices, body(): lax.psum_scatter(lax.dot_general(grad_pre, effective, (((1,), (1,)), ((),...  88.3 us
    all_to_all x1, waiting for transfers between devices, body(): lax.all_to_all(cotangent[0], 'fsdp', split_axis=1, concat_axis=0, tiled=T...  81.1 us
    reduce_scatter x1, waiting for transfers between devices, body(): lax.psum_scatter((scaled * domain_weight[0].astype(jnp.float32)).astype(j...  54 us
    unnamed x7, local copies, waits for them, and re-layouts  44.1 us
    dot_general x1, matrix products, body(): lax.dot_general(piece, fold_grad_pre, (((0,), (0,)), ((), ())), preferred...  20.9 us
    dot_general x1, matrix products, body(): lax.dot_general(grad_pre, effective, (((1,), (1,)), ((), ())), preferred_...  17.8 us
    dot_general x1, matrix products, body(): preact = jnp.dot(piece, effective, preferred_element_type=jnp.float32)  17.1 us
    all_gather x1, waiting for transfers between devices, body(): piece = lax.all_gather(inputs[0], 'fsdp', axis=0, tiled=True)  13.7 us
  transfers between devices with their start and end apart: 4, of which 4 were waited for; matrix products, arithmetic and copies ran while one was open for 17% of the time, Pallas kernels for 0%

commit v1 on v0

--- a/solution.py
+++ b/solution.py
@@ -9,7 +9,11 @@
         jnp.bfloat16
     )
     live_rows = row_counts[0]
-    columns = lax.all_to_all(cotangent[0], "fsdp", split_axis=1, concat_axis=0, tiled=True)
+    own = cotangent[0]
+    size = lax.axis_size("fsdp")
+    tiles = jnp.stack(jnp.split(own, size, axis=1), axis=0)
+    tiles = lax.all_to_all(tiles, "fsdp", split_axis=0, concat_axis=0)
+    columns = jnp.concatenate(tiles, axis=0)
     piece = lax.all_gather(inputs[0], "fsdp", axis=0, tiled=True)
     length = piece.shape[0]
     upstream = columns.astype(jnp.float32)

time: 360 us -> 363 us (level)
  waiting for transfers between devices: 238 us -> 223 us
  local copies, waits for them, and re-layouts: 44.1 us -> 58.5 us
    all_gather x1, waiting for transfers between devices: 13.7 us -> 1.49 us  [body(): piece = lax.all_gather(inputs[0], 'fsdp', axis=0, tiled=True)]
    unnamed x7 -> x11, local copies, waits for them, and re-layouts: 44.1 us -> 51.4 us
    convert_element_type x0 -> x1, local copies, waits for them, and re-layouts: none -> 5.44 us  [body(): upstream = columns.astype(jnp.float32)]
    all_to_all x1, waiting for transfers between devices: 81.1 us -> 77.5 us  [body(): tiles = lax.all_to_all(tiles, 'fsdp', split_axis=0, concat_axis=0)]
  transfers between devices with their start and end apart: 4 -> 4, of which waited for: 4 -> 4; matrix products, arithmetic and copies ran while one was open for 17% -> 22% of each run, Pallas kernels for 0% -> 0%
where the time goes in v1:
time: 363 us; the launch traced here: 361 us
  waiting for transfers between devices  223 us (61%)
  local copies, waits for them, and re-layouts  58.5 us (16%)
  matrix products  56.4 us (16%)
  between operations  14.4 us (4%)
  starting transfers between devices  6.65 us (2%)
    reduce_scatter x1, waiting for transfers between devices, body(): lax.psum_scatter(lax.dot_general(grad_pre, effective, (((1,), (1,)), ((),...  88.3 us
    all_to_all x1, waiting for transfers between devices, body(): tiles = lax.all_to_all(tiles, 'fsdp', split_axis=0, concat_axis=0)  77.5 us
    reduce_scatter x1, waiting for transfers between devices, body(): lax.psum_scatter((scaled * domain_weight[0].astype(jnp.float32)).astype(j...  54.6 us
    unnamed x11, local copies, waits for them, and re-layouts  51.4 us
    dot_general x1, matrix products, body(): lax.dot_general(piece, fold_grad_pre, (((0,), (0,)), ((), ())), preferred...  19.5 us
    dot_general x1, matrix products, body(): preact = jnp.dot(piece, effective, preferred_element_type=jnp.float32)  19 us
    dot_general x1, matrix products, body(): lax.dot_general(grad_pre, effective, (((1,), (1,)), ((), ())), preferred_...  17.8 us
  transfers between devices with their start and end apart: 4, of which 4 were waited for; matrix products, arithmetic and copies ran while one was open for 22% of the time, Pallas kernels for 0%

profile of v1, /device:TPU:0, one launch (start us, length us, event | category | flops | bytes accessed | tf_op | source)
XLA Modules:
  0.0 361.2 jit_solution(13402438352389351388)
XLA Ops:
  7.2 0.0 all-gather.3.cloned.1.call-start
  7.2 0.7 all-gather.3.cloned.1.call-update
  7.9 1.7 fusion.26
  9.6 1.7 fusion.25
  11.2 1.7 fusion.24
  12.9 1.7 fusion.23
  14.6 1.7 fusion.22
  16.2 1.7 fusion.21
  17.9 1.7 fusion.20
  19.6 1.7 fusion.19
  21.3 6.3 %all-to-all-start = ((bf16[8,128,1024]{2,1,0:T(8,128)(2,1)}), bf16[8,128,1024]{2,1,0:T(8,128)(2,1)S(1)}, u32[]{:S(2)}, u32[]{:S(2)}) async-start(bf16[8,128,1024]{2,1,0:T(8,128)(2,1)} %fusion.19), calls=%async_computation | async-start | bytes 4194304 | tf_op jit(solution)/shard_map/all_to_all | solution.py:15
  27.7 0.0 reduce-scatter.3.cloned.1.call-start
  28.4 11.9 %copy.9 = bf16[4096,1024]{0,1:T(8,128)(2,1)} copy(bf16[4096,1024]{1,0:T(8,128)(2,1)} %param.7) | data formatting | bytes 16777216 | tf_op args[2]
  40.3 11.5 %copy.10 = bf16[1,4096,1024]{1,2,0:T(8,128)(2,1)} copy(bf16[1,4096,1024]{2,1,0:T(8,128)(2,1)} %param.8) | data formatting | bytes 16777216 | tf_op args[3]
  51.9 77.5 %all-to-all-done = bf16[8,128,1024]{2,1,0:T(8,128)(2,1)S(1)} async-done(((bf16[8,128,1024]{2,1,0:T(8,128)(2,1)}), bf16[8,128,1024]{2,1,0:T(8,128)(2,1)S(1)}, u32[]{:S(2)}, u32[]{:S(2)}) %all-to-all-start) | async-done | bytes 2097184 | tf_op jit(solution)/shard_map/all_to_all | solution.py:15
  129.3 2.6 bitcast_convert_fusion
  131.9 5.4 %copy.13 = f32[1024,1024]{0,1:T(8,128)} copy(f32[1024,1024]{1,0:T(8,128)} %bitcast_convert_fusion) | data formatting | bytes 8388608 | tf_op jit(solution)/shard_map/convert_element_type | solution.py:19
  137.4 1.5 all-gather.3.cloned.1.call-done
  138.9 19.0 %fusion.14 = bf16[1024,1024]{0,1:T(8,128)(2,1)S(1)} fusion(f32[1024,1024]{0,1:T(8,128)} %copy.13, bf16[1,1024,4096]{2,1,0:T(8,128)(2,1)} %all-gather.3.cloned.1.call-done, bf16[4096,1024]{0,1:T(8,128)(2,1)} %copy.9, bf16[1,4096,1024]{1,2,0:T(8,128)(2,1)} %copy.10, pred[1024]{0:T(1024)(128)(4,1)S(1)} %iota_compare_fusion), kind=kOutput, calls=%fused_computation.20 | convolution fusion | flops 8617197568 | bytes 31458304 | tf_op jit(solution)/shard_map/dot_general | solution.py:20
  157.9 19.5 %fusion.3 = (bf16[1,4096,1024]{1,2,0:T(8,128)(2,1)}, bf16[4096,1024]{0,1:T(8,128)(2,1)}) fusion(bf16[4096,1024]{0,1:T(8,128)(2,1)} %copy.9, f32[]{:T(128)S(6)} %rsqrt.3, bf16[1,4096,1024]{1,2,0:T(8,128)(2,1)} %copy.10, bf16[1024,1024]{0,1:T(8,128)(2,1)S(1)} %fusion.14, bf16[1,1024,4096]{2,1,0:T(8,128)(2,1)} %all-gather.3.cloned.1.call-done), kind=kOutput, calls=%fused_computation.6 | convolution fusion | flops 8619294720 | bytes 44040196 | tf_op jit(solution)/shard_map/dot_general | solution.py:27
  177.4 0.0 reduce-scatter.3.cloned.1.call-update
  177.4 0.2 reduce-scatter.5.cloned.1.call-start
  177.7 17.8 %convolution_convert_fusion = bf16[1024,4096]{1,0:T(8,128)(2,1)} fusion(bf16[1024,1024]{0,1:T(8,128)(2,1)S(1)} %fusion.14, bf16[4096,1024]{0,1:T(8,128)(2,1)} %copy.9, bf16[1,4096,1024]{1,2,0:T(8,128)(2,1)} %copy.10), kind=kOutput, calls=%fused_computation.11 | convolution fusion | flops 8610906112 | bytes 27262976 | tf_op jit(solution)/shard_map/dot_general | solution.py:33
  195.5 0.0 reduce-scatter.5.cloned.1.call-update
  195.5 12.1 %copy.12 = bf16[1,4096,1024]{2,1,0:T(8,128)(2,1)} copy(bf16[1,4096,1024]{1,2,0:T(8,128)(2,1)} %get-tuple-element.6) | data formatting | bytes 16777216
  207.6 54.6 %reduce-scatter.3.cloned.1.call-done = bf16[1024,1024]{0,1:T(8,128)(2,1)} async-done(((bf16[4096,1024]{0,1:T(8,128)(2,1)}), bf16[1024,1024]{0,1:T(8,128)(2,1)}) %reduce-scatter.3.cloned.1.call-update) | async-done | bytes 2097168 | tf_op jit(solution)/shard_map/reduce_scatter | solution.py:40
  262.3 4.1 %copy.11 = f32[1024,1024]{1,0:T(8,128)} copy(bf16[1024,1024]{0,1:T(8,128)(2,1)} %reduce-scatter.3.cloned.1.call-done) | data formatting | bytes 6291456
  266.4 88.3 %reduce-scatter.5.cloned.1.call-done = bf16[128,4096]{1,0:T(8,128)(2,1)} async-done(((bf16[1024,4096]{1,0:T(8,128)(2,1)}), bf16[128,4096]{1,0:T(8,128)(2,1)}) %reduce-scatter.5.cloned.1.call-update) | async-done | bytes 1048592 | tf_op jit(solution)/shard_map/reduce_scatter | solution.py:32
  (1 shorter events, 0.0 us)
Async XLA Ops:
  7.2 131.7 %all-gather.3.cloned.1.call-start = ((), (), s32[]{:S(2)}) async-start(), calls=%async_computation.5 | async-start | bytes 9437184 | tf_op jit(solution)/shard_map/all_gather | solution.py:17
  21.3 108.0 %all-to-all-start = ((bf16[8,128,1024]{2,1,0:T(8,128)(2,1)}), bf16[8,128,1024]{2,1,0:T(8,128)(2,1)S(1)}, u32[]{:S(2)}, u32[]{:S(2)}) async-start(bf16[8,128,1024]{2,1,0:T(8,128)(2,1)} %fusion.19), calls=%async_computation | async-start | bytes 4194304 | tf_op jit(solution)/shard_map/all_to_all | solution.py:15
  27.7 234.6 %reduce-scatter.3.cloned.1.call-start = ((), (), s32[]{:S(2)}) async-start(), calls=%async_computation.3 | async-start | bytes 10485760 | tf_op jit(solution)/shard_map/reduce_scatter | solution.py:40
  177.4 177.2 %reduce-scatter.5.cloned.1.call-start = ((), (), s32[]{:S(2)}) async-start(), calls=%async_computation.4 | async-start | bytes 9437184 | tf_op jit(solution)/shard_map/reduce_scatter | solution.py:32
Sparse Core Ops, SparseCore 0:
  9.6 129.2 all-gather.2
  177.6 84.6 reduce-scatter.2
  265.1 89.4 reduce-scatter.4
